TPU v7x, 32 devices: a whole 2x2x4 slice. The times are simulated.
32 devices in a mesh: sub: 4 (over y, core), row: 2 (over x), col: 4 (over z).
Axes of the slice: x: 2, y: 2, z: 4, core: 2. Of those that a mesh axis runs over, the one named last changes fastest.
Arguments:
- inverse_quarter: bfloat16 [4, 8192, 8192], P('sub', 'row', 'col'), may hold values from -1 to 3
- inverse_half: bfloat16 [4, 8192, 4096], P('sub', 'row', 'col'), may hold values from -1 to 3
- inverse_root: bfloat16 [16384, 16384], P('row', ('sub', 'col')), may hold values from -1 to 3
- quarter_to_half: bfloat16 [4, 2, 4096, 8192], P('sub', None, 'col', 'row'), may hold values from -0.0625 to 0.0625
- quarter_to_root: bfloat16 [4, 2, 4096, 8192], P('sub', None, 'col', 'row'), may hold values from -0.0625 to 0.0625
- half_to_root: bfloat16 [4, 2, 4096, 8192], P('sub', None, 'col', 'row'), may hold values from -0.0625 to 0.0625
- right_quarter: bfloat16 [4, 8192, 256], P('sub', 'col'), may hold values from -6 to 6
- right_half: bfloat16 [4, 4096, 256], P('sub', 'col'), may hold values from -6 to 6
- right_root: bfloat16 [16384, 256], P(('sub', 'col')), may hold values from -6 to 6
- row_blocks: int32 [3, 4, 2, 16], replicated, may hold values 0 or 1
Outputs:
- quarter_solution: float32 [4, 8192, 256], P('sub', 'col', 'row')
- half_solution: bfloat16 [4, 4096, 256], P('sub', 'col')
- root_solution: bfloat16 [16384, 256], P(('sub', 'col'))
All inputs are finite; a program needn't handle non-finite values.
Results may differ from a plain program's by a relative error of at most 0.01.
Values may be sent and summed in bfloat16 or wider, within the bound.
No kernel may reach another device: no remote copies, remote signals or barrier semaphores. Data moves between devices by JAX's collectives and lax.ppermute only.
A program may use at most 256 MiB of HBM per device.

v0:
```python
import jax
import jax.numpy as jnp
from jax import lax
from jax.sharding import PartitionSpec as P

BLK = 256


def from_partner(array, axis, stride):
    return lax.ppermute(array, axis, [(i, i ^ 1 << stride) for i in range(lax.axis_size(axis))])


def sum_rows(values):
    return lax.psum(values, "row")


def sum_columns(values):
    return lax.psum(values, "col")


def partner(values, bit):
    return from_partner(values, "sub", bit)


def partner_solution(values, bit):
    return from_partner(values, "sub", bit)


def project(matrix, vector):
    halves, height, inner = matrix.shape
    flat = jnp.dot(
        matrix.reshape(halves * height, inner), vector, preferred_element_type=jnp.float32
    )
    return flat.reshape(halves, height, vector.shape[1])


def project_back(matrix, pieces):
    inner = matrix.shape[2]
    return lax.dot_general(
        matrix.reshape(-1, inner),
        pieces.reshape(-1, pieces.shape[2]),
        (((0,), (0,)), ((), ())),
        preferred_element_type=jnp.float32,
    )


def transposed(matrix, vector):
    return lax.dot_general(
        matrix, vector, (((0,), (0,)), ((), ())), preferred_element_type=jnp.float32
    )


def pair_reduce(partial_value, bit, own_bit):
    totals = sum_rows(partial_value)
    own_piece = lax.dynamic_index_in_dim(totals, own_bit, 0, keepdims=False)
    other_piece = lax.dynamic_index_in_dim(totals, 1 - own_bit, 0, keepdims=False)
    return own_piece + partner(other_piece, bit)


def order_pair(own_piece, other_piece, own_bit):
    return jnp.where(
        own_bit == 0, jnp.stack([own_piece, other_piece]), jnp.stack([other_piece, own_piece])
    )


def per_device(
    inverse_quarter,
    inverse_half,
    inverse_root,
    quarter_to_half,
    quarter_to_root,
    half_to_root,
    right_quarter,
    right_half,
    right_root,
    row_blocks,
):
    sub_index = lax.axis_index("sub")
    column_index = lax.axis_index("col")
    low_bit = sub_index % 2
    high_bit = sub_index // 2
    piece_rows = quarter_to_half.shape[2]
    block_count = piece_rows // BLK
    row_flags = lax.dynamic_slice(
        row_blocks,
        (jnp.int32(0), sub_index, jnp.int32(0), column_index * block_count),
        (3, 1, 2, block_count),
    )[:, 0]
    masking = jnp.repeat(row_flags, BLK, axis=2).astype(jnp.float32)[:, :, :, None]
    mask_half = masking[0]
    mask_root = masking[1]
    mask_upper = masking[2]
    solved_quarter = sum_columns(
        jnp.dot(inverse_quarter[0], right_quarter[0], preferred_element_type=jnp.float32)
    ).astype(jnp.bfloat16)
    half_part = project(quarter_to_half[0], solved_quarter) * mask_half
    root_part = project(quarter_to_root[0], solved_quarter) * mask_root
    half_terms = pair_reduce(half_part, 0, low_bit)
    root_early = pair_reduce(root_part, 1, high_bit)
    half_right = (right_half[0].astype(jnp.float32) - half_terms).astype(jnp.bfloat16)
    half_sum = sum_columns(jnp.dot(inverse_half[0], half_right, preferred_element_type=jnp.float32))
    solved_half = (half_sum + partner(half_sum, 0)).astype(jnp.bfloat16)
    upper_part = project(half_to_root[0], solved_half) * mask_upper
    root_terms = root_early + pair_reduce(upper_part, 1, high_bit)
    root_right = (right_root.astype(jnp.float32) - root_terms).astype(jnp.bfloat16)
    solved_root = lax.psum(
        jnp.dot(inverse_root, root_right, preferred_element_type=jnp.float32), ("sub", "col")
    ).astype(jnp.bfloat16)
    root_solution = sum_rows(transposed(inverse_root, solved_root)).astype(jnp.bfloat16)
    root_other = partner_solution(root_solution, 1)
    root_pieces = order_pair(root_solution, root_other, high_bit)
    upper_back = project_back(half_to_root[0], root_pieces * mask_upper.astype(jnp.bfloat16))
    quarter_root_back = project_back(
        quarter_to_root[0], root_pieces * mask_root.astype(jnp.bfloat16)
    )
    upper_sum, quarter_root_sum = sum_columns((upper_back, quarter_root_back))
    upper_total = upper_sum + partner(upper_sum, 0)
    half_update = (solved_half.astype(jnp.float32) - upper_total).astype(jnp.bfloat16)
    half_solution = sum_rows(transposed(inverse_half[0], half_update)).astype(jnp.bfloat16)
    half_other = partner_solution(half_solution, 0)
    half_pieces = order_pair(half_solution, half_other, low_bit)
    quarter_half_back = project_back(
        quarter_to_half[0], half_pieces * mask_half.astype(jnp.bfloat16)
    )
    quarter_total = quarter_root_sum + sum_columns(quarter_half_back)
    quarter_update = (solved_quarter.astype(jnp.float32) - quarter_total).astype(jnp.bfloat16)
    quarter_solution = lax.psum_scatter(
        transposed(inverse_quarter[0], quarter_update), "row", scatter_dimension=1, tiled=True
    )
    return (quarter_solution[None], half_solution[None], root_solution)


def solution(mesh):
    placed = (
        P("sub", "row", "col"),
        P("sub", "row", "col"),
        P("row", ("sub", "col")),
        P("sub", None, "col", "row"),
        P("sub", None, "col", "row"),
        P("sub", None, "col", "row"),
        P("sub", "col", None),
        P("sub", "col", None),
        P(("sub", "col"), None),
        P(),
    )
    return jax.shard_map(
        per_device,
        mesh=mesh,
        in_specs=placed,
        out_specs=(P("sub", "col", "row"), P("sub", "col", None), P(("sub", "col"), None)),
        check_vma=False,
    )
```

profile of v0, /device:TPU:0, one launch (start us, length us, event | category | flops | bytes accessed | tf_op | source)
XLA Modules:
  0.0 1504.3 jit_solution(598691174003169941)
XLA Ops:
  8.4 10.1 fusion.2
  18.5 148.8 %all-reduce.20 = bf16[4096,256]{1,0:T(8,128)(2,1)S(1)} all-reduce(f32[4096,256]{1,0:T(8,128)} %fusion.2), channel_id=1, replica_groups=mesh['sub'=4,'row'=2,'col'=4] {'col'}, use_global_device_ids=true, to_apply=%region_0.1 | all-reduce | flops 1048576 | bytes 6291456 | tf_op jit(solution)/shard_map/psum | solution.py:18
  167.3 9.5 convolution_bitcast_fusion.3
  176.8 4.0 reshape.180
  184.7 61.4 %all-reduce.11.cloned.1.call-done = f32[2,1024,256]{1,0,2:T(2,128)} async-done(((f32[2,1024,256]{1,0,2:T(2,128)}), f32[2,1024,256]{1,0,2:T(2,128)}) %all-reduce.11.cloned.1.call-update) | async-done | bytes 2097168 | tf_op jit(solution)/shard_map/psum | solution.py:14
  246.1 5.3 constant_dynamic-slice_fusion.3
  258.0 8.6 fusion.9
  266.9 154.9 %all-reduce.13.cloned.1.call-done = f32[4096,256]{0,1:T(8,128)} async-done(((f32[4096,256]{0,1:T(8,128)}), f32[4096,256]{0,1:T(8,128)}) %all-reduce.13.cloned.1.call-update) | async-done | bytes 4194320 | tf_op jit(solution)/shard_map/psum | solution.py:18
  421.9 9.6 convolution_bitcast_fusion.4
  431.4 4.0 reshape.179
  438.8 4.1 add_convert_fusion
  442.9 12.3 convolution_bitcast_fusion.2
  455.2 4.0 reshape.181
  463.0 107.1 %all-reduce.19.cloned.1.call-done = (f32[2,1024,256]{1,0,2:T(2,128)}, f32[2,1024,256]{1,0,2:T(2,128)}) async-done(((f32[2,1024,256]{1,0,2:T(2,128)}, f32[2,1024,256]{1,0,2:T(2,128)}), (f32[2,1024,256]{1,0,2:T(2,128)}, f32[2,1024,256]{1,0,2:T(2,128)})) %all-reduce.19.cloned.1.call-update) | async-done | bytes 4194320 | tf_op jit(solution)/shard_map/psum | solution.py:14
  570.1 5.5 constant_dynamic-slice_fusion.1
  592.4 18.4 %collective-permute-done = f32[1024,256]{1,0:T(8,128)} collective-permute-done((f32[1024,256]{1,0:T(8,128)}, f32[1024,256]{1,0:T(8,128)}, u32[]{:S(2)}, u32[]{:S(2)}) %collective-permute-start) | collective-permute-done | bytes 1048608 | tf_op jit(solution)/shard_map/ppermute | solution.py:10
  610.8 21.3 %collective-permute-done.3 = f32[1024,256]{1,0:T(8,128)} collective-permute-done((f32[1024,256]{1,0:T(8,128)}, f32[1024,256]{1,0:T(8,128)}, u32[]{:S(2)}, u32[]{:S(2)}) %collective-permute-start.3) | collective-permute-done | bytes 1048608 | tf_op jit(solution)/shard_map/ppermute | solution.py:10
  632.1 11.5 convolution_bitcast_fusion
  643.6 350.3 %all-reduce.21 = bf16[8192,256]{0,1:T(8,128)(2,1)} all-reduce(f32[8192,256]{0,1:T(8,128)} %convolution_bitcast_fusion), channel_id=1, replica_groups=mesh['sub'=4,'row'=2,'col'=4] {'sub','col'}, use_global_device_ids=true, to_apply=%region_5.6 | all-reduce | flops 2097152 | bytes 12582912 | tf_op jit(solution)/shard_map/psum | solution.py:106
  993.9 12.5 fusion.17
  1006.4 28.8 %all-reduce.22 = bf16[1024,256]{0,1:T(8,128)(2,1)S(1)} all-reduce(f32[1024,256]{0,1:T(8,128)} %fusion.17), channel_id=1, replica_groups=mesh['sub'=4,'row'=2,'col'=4] {'row'}, use_global_device_ids=true, to_apply=%region_6.7 | all-reduce | flops 262144 | bytes 1572864 | tf_op jit(solution)/shard_map/psum | solution.py:14
  1035.6 11.8 collective-permute-done.4
  1050.5 10.1 convolution_bitcast_fusion.1
  1060.7 157.8 %all-reduce.15.cloned.1.call-done = f32[4096,256]{0,1:T(8,128)} async-done(((f32[4096,256]{0,1:T(8,128)}), f32[4096,256]{0,1:T(8,128)}) %all-reduce.15.cloned.1.call-update) | async-done | bytes 4194320 | tf_op jit(solution)/shard_map/psum | solution.py:18
  1219.8 6.2 collective-permute-done.5
  1226.0 9.9 fusion.20
  1235.8 30.3 %all-reduce.23 = bf16[1024,256]{0,1:T(8,128)(2,1)S(1)} all-reduce(f32[1024,256]{0,1:T(8,128)} %fusion.20), channel_id=1, replica_groups=mesh['sub'=4,'row'=2,'col'=4] {'row'}, use_global_device_ids=true, to_apply=%region_9.10 | all-reduce | flops 262144 | bytes 1572864 | tf_op jit(solution)/shard_map/psum | solution.py:14
  1266.3 14.8 fusion.35
  1283.7 13.7 fusion.8
  1297.7 153.0 %all-reduce.17.cloned.1.call-done = f32[4096,256]{1,0:T(8,128)} async-done(((f32[4096,256]{1,0:T(8,128)}), f32[4096,256]{1,0:T(8,128)}) %all-reduce.17.cloned.1.call-update) | async-done | bytes 4194320 | tf_op jit(solution)/shard_map/psum | solution.py:18
  1450.7 13.0 fusion.14
  1467.8 26.9 %reduce-scatter.2.cloned.1.call-done = f32[2048,128]{0,1:T(8,128)} async-done(((f32[2048,256]{0,1:T(8,128)}), f32[2048,128]{0,1:T(8,128)}) %reduce-scatter.2.cloned.1.call-update) | async-done | bytes 1048592 | tf_op jit(solution)/shard_map/reduce_scatter | solution.py:127
  (67 shorter events, 50.3 us)
Async XLA Ops:
  7.2 1.2 copy-start
  7.2 238.9 %all-reduce.11.cloned.1.call-start = ((), (), s32[]{:S(2)}) async-start(), calls=%async_computation.1 | async-start | bytes 4194304 | tf_op jit(solution)/shard_map/psum | solution.py:14
  184.1 237.7 %all-reduce.13.cloned.1.call-start = ((), (), s32[]{:S(2)}) async-start(), calls=%async_computation.2 | async-start | bytes 8388608 | tf_op jit(solution)/shard_map/psum | solution.py:18
  255.0 3.0 collective-permute-start.1
  266.6 303.4 %all-reduce.19.cloned.1.call-start = ((), (), s32[]{:S(2)}) async-start(), calls=%async_computation.6 | async-start | bytes 8388608 | tf_op jit(solution)/shard_map/psum | solution.py:14
  421.8 17.1 %collective-permute-start.2 = (f32[4096,256]{0,1:T(8,128)}, f32[4096,256]{0,1:T(8,128)}, u32[]{:S(2)}, u32[]{:S(2)}) collective-permute-start(f32[4096,256]{0,1:T(8,128)} %all-reduce.13.cloned.1.call-done), channel_id=1, source_target_pairs={{0,8},{8,0},{16,24},{24,16},{1,9},{9,1},{17,25},{25,17},{2,10},{10... | collective-permute-start | bytes 12582920 | tf_op jit(solution)/shard_map/ppermute | solution.py:10
  435.4 3.4 copy-start.4
  462.5 756.0 %all-reduce.15.cloned.1.call-start = ((), (), s32[]{:S(2)}) async-start(), calls=%async_computation.3 | async-start | bytes 8388608 | tf_op jit(solution)/shard_map/psum | solution.py:18
  570.1 5.5 copy-start.6
  584.4 26.4 %collective-permute-start = (f32[1024,256]{1,0:T(8,128)}, f32[1024,256]{1,0:T(8,128)}, u32[]{:S(2)}, u32[]{:S(2)}) collective-permute-start(f32[1024,256]{1,0:T(8,128)} %bitcast.6), channel_id=1, source_target_pairs={{0,16},{8,24},{16,0},{24,8},{1,17},{9,25},{17,1},{25,9},{2,18},{10... | collective-permute-start | bytes 3145736 | tf_op jit(solution)/shard_map/ppermute | solution.py:10
  585.9 46.2 %collective-permute-start.3 = (f32[1024,256]{1,0:T(8,128)}, f32[1024,256]{1,0:T(8,128)}, u32[]{:S(2)}, u32[]{:S(2)}) collective-permute-start(f32[1024,256]{1,0:T(8,128)} %bitcast.138), channel_id=1, source_target_pairs={{0,16},{8,24},{16,0},{24,8},{1,17},{9,25},{17,1},{25,9},{2,18},{10... | collective-permute-start | bytes 3145736 | tf_op jit(solution)/shard_map/ppermute | solution.py:10
  1035.2 13.8 copy-start.3
  1035.2 12.1 collective-permute-start.4
  1060.6 157.9 %copy-start.5 = (bf16[2,1024,256]{1,2,0:T(8,128)(2,1)S(1)}, bf16[2,1024,256]{1,2,0:T(8,128)(2,1)}, u32[]{:S(2)}) copy-start(bf16[2,1024,256]{1,2,0:T(8,128)(2,1)} %get-tuple-element.18) | copy-start | bytes 3145732
  1060.7 390.1 %all-reduce.17.cloned.1.call-start = ((), (), s32[]{:S(2)}) async-start(), calls=%async_computation.5 | async-start | bytes 8388608 | tf_op jit(solution)/shard_map/psum | solution.py:18
  1218.5 7.5 collective-permute-start.5
  1266.2 14.9 copy-start.2
  1266.2 14.9 collective-permute-start.6
  1297.5 197.2 %reduce-scatter.2.cloned.1.call-start = ((), (), s32[]{:S(2)}) async-start(), calls=%async_computation.4 | async-start | bytes 3145728 | tf_op jit(solution)/shard_map/reduce_scatter | solution.py:127
  1450.7 46.5 %copy-start.1 = (bf16[1,2048,256]{2,1,0:T(8,128)(2,1)S(1)}, bf16[1,2048,256]{2,1,0:T(8,128)(2,1)}, u32[]{:S(2)}) copy-start(bf16[1,2048,256]{2,1,0:T(8,128)(2,1)} %param.16) | copy-start | bytes 3145732
Sparse Core Ops, SparseCore 0:
  184.2 61.8 all-reduce.10
  266.8 154.9 all-reduce.12
  462.6 107.3 all-reduce.18
  1060.8 157.6 all-reduce.14
  1297.6 153.0 all-reduce.16
  1463.8 30.8 reduce-scatter.1
where the time goes:
time: 1510 us; the launch traced here: 1500 us
  waiting for transfers between devices  720 us (48%)
  blocking collectives  558 us (37%)
  matrix products  135 us (9%)
  local copies, waits for them, and re-layouts  54.8 us (4%)
  other arithmetic  17.5 us (1%)
    psum x3, waiting for transfers between devices, sum_columns(): return lax.psum(values, 'col')  466 us
    psum x1, blocking collectives, per_device(): lax.psum(jnp.dot(inverse_root, root_right, preferred_element_type=jnp.flo...  350 us
    psum x2, waiting for transfers between devices, sum_rows(): return lax.psum(values, 'row')  168 us
    psum x1, blocking collectives, sum_columns(): return lax.psum(values, 'col')  149 us
    psum x2, blocking collectives, sum_rows(): return lax.psum(values, 'row')  59.1 us
    ppermute x7, waiting for transfers between devices, from_partner(): lax.ppermute(array, axis, [(i, i ^ 1 << stride) for i in range(lax.axis_s...  58.6 us
    dot_general x3, matrix products, project_back(): lax.dot_general(matrix.reshape(-1, inner), pieces.reshape(-1, pieces.shap...  38.7 us
    dot_general x3, matrix products, transposed(): lax.dot_general(matrix, vector, (((0,), (0,)), ((), ())), preferred_eleme...  35.3 us
  transfers between devices with their start and end apart: 13, of which 11 were waited for; matrix products, arithmetic and copies ran while one was open for 3% of the time, Pallas kernels for 0%

commit v1 on v0

--- a/solution.py
+++ b/solution.py
@@ -104,7 +104,8 @@
     root_terms = root_early + pair_reduce(upper_part, 1, high_bit)
     root_right = (right_root.astype(jnp.float32) - root_terms).astype(jnp.bfloat16)
     solved_root = lax.psum(
-        jnp.dot(inverse_root, root_right, preferred_element_type=jnp.float32), ("sub", "col")
+        lax.psum(jnp.dot(inverse_root, root_right, preferred_element_type=jnp.float32), "col"),
+        "sub",
     ).astype(jnp.bfloat16)
     root_solution = sum_rows(transposed(inverse_root, solved_root)).astype(jnp.bfloat16)
     root_other = partner_solution(root_solution, 1)

time: 1510 us -> 1600 us (1.060)
  waiting for transfers between devices: 720 us -> 1010 us
  blocking collectives: 558 us -> 358 us
    psum x0 -> x1, waiting for transfers between devices: none -> 291 us  [per_device(): lax.psum(jnp.dot(inverse_root, root_right, preferred_element_type=jnp.flo...]
    psum x1, blocking collectives: 350 us -> 148 us  [per_device(): lax.psum(lax.psum(jnp.dot(inverse_root, root_right, preferred_element_typ...]
  transfers between devices with their start and end apart: 13 -> 14, of which waited for: 11 -> 12; matrix products, arithmetic and copies ran while one was open for 3% -> 3% of each run, Pallas kernels for 0% -> 0%
where the time goes in v1:
time: 1600 us; the launch traced here: 1590 us
  waiting for transfers between devices  1010 us (63%)
  blocking collectives  358 us (22%)
  matrix products  135 us (8%)
  local copies, waits for them, and re-layouts  54.8 us (3%)
  other arithmetic  17.5 us (1%)
    psum x3, waiting for transfers between devices, sum_columns(): return lax.psum(values, 'col')  460 us
    psum x1, waiting for transfers between devices, per_device(): lax.psum(jnp.dot(inverse_root, root_right, preferred_element_type=jnp.flo...  291 us
    psum x2, waiting for transfers between devices, sum_rows(): return lax.psum(values, 'row')  168 us
    psum x1, blocking collectives, sum_columns(): return lax.psum(values, 'col')  149 us
    psum x1, blocking collectives, per_device(): lax.psum(lax.psum(jnp.dot(inverse_root, root_right, preferred_element_typ...  148 us
    psum x2, blocking collectives, sum_rows(): return lax.psum(values, 'row')  61.3 us
    ppermute x7, waiting for transfers between devices, from_partner(): lax.ppermute(array, axis, [(i, i ^ 1 << stride) for i in range(lax.axis_s...  59 us
    dot_general x3, matrix products, project_back(): lax.dot_general(matrix.reshape(-1, inner), pieces.reshape(-1, pieces.shap...  38.7 us
  transfers between devices with their start and end apart: 14, of which 12 were waited for; matrix products, arithmetic and copies ran while one was open for 3% of the time, Pallas kernels for 0%

profile of v1, /device:TPU:0, one launch (start us, length us, event | category | flops | bytes accessed | tf_op | source)
XLA Modules:
  0.0 1589.9 jit_solution(15064084745001231884)
XLA Ops:
  8.4 10.1 fusion.2
  18.5 148.8 %all-reduce.23 = bf16[4096,256]{1,0:T(8,128)(2,1)S(1)} all-reduce(f32[4096,256]{1,0:T(8,128)} %fusion.2), channel_id=1, replica_groups=mesh['sub'=4,'row'=2,'col'=4] {'col'}, use_global_device_ids=true, to_apply=%region_0.1 | all-reduce | flops 1048576 | bytes 6291456 | tf_op jit(solution)/shard_map/psum | solution.py:18
  167.3 9.5 convolution_bitcast_fusion.3
  176.8 4.0 reshape.180
  184.7 61.4 %all-reduce.12.cloned.1.call-done = f32[2,1024,256]{1,0,2:T(2,128)} async-done(((f32[2,1024,256]{1,0,2:T(2,128)}), f32[2,1024,256]{1,0,2:T(2,128)}) %all-reduce.12.cloned.1.call-update) | async-done | bytes 2097168 | tf_op jit(solution)/shard_map/psum | solution.py:14
  246.1 5.3 constant_dynamic-slice_fusion.3
  258.0 8.6 fusion.9
  266.9 154.9 %all-reduce.14.cloned.1.call-done = f32[4096,256]{0,1:T(8,128)} async-done(((f32[4096,256]{0,1:T(8,128)}), f32[4096,256]{0,1:T(8,128)}) %all-reduce.14.cloned.1.call-update) | async-done | bytes 4194320 | tf_op jit(solution)/shard_map/psum | solution.py:18
  421.9 9.6 convolution_bitcast_fusion.4
  431.4 4.0 reshape.179
  438.8 4.1 add_convert_fusion
  442.9 12.3 convolution_bitcast_fusion.2
  462.9 107.1 %all-reduce.22.cloned.1.call-done = (f32[2,1024,256]{1,0,2:T(2,128)}, f32[2,1024,256]{1,0,2:T(2,128)}) async-done(((f32[2,1024,256]{1,0,2:T(2,128)}, f32[2,1024,256]{1,0,2:T(2,128)}), (f32[2,1024,256]{1,0,2:T(2,128)}, f32[2,1024,256]{1,0,2:T(2,128)})) %all-reduce.22.cloned.1.call-update) | async-done | bytes 4194320 | tf_op jit(solution)/shard_map/psum | solution.py:14
  570.0 5.5 constant_dynamic-slice_fusion.1
  592.4 18.4 %collective-permute-done = f32[1024,256]{1,0:T(8,128)} collective-permute-done((f32[1024,256]{1,0:T(8,128)}, f32[1024,256]{1,0:T(8,128)}, u32[]{:S(2)}, u32[]{:S(2)}) %collective-permute-start) | collective-permute-done | bytes 1048608 | tf_op jit(solution)/shard_map/ppermute | solution.py:10
  610.8 21.3 %collective-permute-done.3 = f32[1024,256]{1,0:T(8,128)} collective-permute-done((f32[1024,256]{1,0:T(8,128)}, f32[1024,256]{1,0:T(8,128)}, u32[]{:S(2)}, u32[]{:S(2)}) %collective-permute-start.3) | collective-permute-done | bytes 1048608 | tf_op jit(solution)/shard_map/ppermute | solution.py:10
  632.1 11.5 convolution_bitcast_fusion
  643.7 290.9 %all-reduce.16.cloned.1.call-done = f32[8192,256]{0,1:T(8,128)} async-done(((f32[8192,256]{0,1:T(8,128)}), f32[8192,256]{0,1:T(8,128)}) %all-reduce.16.cloned.1.call-update) | async-done | bytes 8388624 | tf_op jit(solution)/shard_map/psum | solution.py:107
  934.6 147.6 %all-reduce.24 = bf16[8192,256]{0,1:T(8,128)(2,1)} all-reduce(f32[8192,256]{0,1:T(8,128)} %all-reduce.16.cloned.1.call-done), channel_id=1, replica_groups=mesh['sub'=4,'row'=2,'col'=4] {'sub'}, use_global_device_ids=true, to_apply=%region_6.7 | all-reduce | flops 2097152 | bytes 12582912 | tf_op jit(solution)/shard_map/psum | solution.py:106
  1082.2 12.5 fusion.17
  1094.7 30.9 %all-reduce.25 = bf16[1024,256]{0,1:T(8,128)(2,1)S(1)} all-reduce(f32[1024,256]{0,1:T(8,128)} %fusion.17), channel_id=1, replica_groups=mesh['sub'=4,'row'=2,'col'=4] {'row'}, use_global_device_ids=true, to_apply=%region_7.8 | all-reduce | flops 262144 | bytes 1572864 | tf_op jit(solution)/shard_map/psum | solution.py:14
  1126.3 12.2 collective-permute-done.4
  1141.6 10.1 convolution_bitcast_fusion.1
  1151.8 152.2 %all-reduce.18.cloned.1.call-done = f32[4096,256]{0,1:T(8,128)} async-done(((f32[4096,256]{0,1:T(8,128)}), f32[4096,256]{0,1:T(8,128)}) %all-reduce.18.cloned.1.call-update) | async-done | bytes 4194320 | tf_op jit(solution)/shard_map/psum | solution.py:18
  1305.4 6.2 collective-permute-done.5
  1311.6 9.9 fusion.20
  1321.4 30.3 %all-reduce.26 = bf16[1024,256]{0,1:T(8,128)(2,1)S(1)} all-reduce(f32[1024,256]{0,1:T(8,128)} %fusion.20), channel_id=1, replica_groups=mesh['sub'=4,'row'=2,'col'=4] {'row'}, use_global_device_ids=true, to_apply=%region_10.11 | all-reduce | flops 262144 | bytes 1572864 | tf_op jit(solution)/shard_map/psum | solution.py:14
  1351.9 14.8 fusion.35
  1369.3 13.7 fusion.8
  1383.3 153.0 %all-reduce.20.cloned.1.call-done = f32[4096,256]{1,0:T(8,128)} async-done(((f32[4096,256]{1,0:T(8,128)}), f32[4096,256]{1,0:T(8,128)}) %all-reduce.20.cloned.1.call-update) | async-done | bytes 4194320 | tf_op jit(solution)/shard_map/psum | solution.py:18
  1536.3 13.0 fusion.14
  1553.4 26.9 %reduce-scatter.2.cloned.1.call-done = f32[2048,128]{0,1:T(8,128)} async-done(((f32[2048,256]{0,1:T(8,128)}), f32[2048,128]{0,1:T(8,128)}) %reduce-scatter.2.cloned.1.call-update) | async-done | bytes 1048592 | tf_op jit(solution)/shard_map/reduce_scatter | solution.py:128
  (70 shorter events, 54.7 us)
Async XLA Ops:
  7.2 1.2 copy-start
  7.2 238.9 %all-reduce.12.cloned.1.call-start = ((), (), s32[]{:S(2)}) async-start(), calls=%async_computation.1 | async-start | bytes 4194304 | tf_op jit(solution)/shard_map/psum | solution.py:14
  184.1 237.7 %all-reduce.14.cloned.1.call-start = ((), (), s32[]{:S(2)}) async-start(), calls=%async_computation.2 | async-start | bytes 8388608 | tf_op jit(solution)/shard_map/psum | solution.py:18
  255.0 3.0 collective-permute-start.1
  266.6 303.4 %all-reduce.22.cloned.1.call-start = ((), (), s32[]{:S(2)}) async-start(), calls=%async_computation.7 | async-start | bytes 8388608 | tf_op jit(solution)/shard_map/psum | solution.py:14
  421.8 17.1 %collective-permute-start.2 = (f32[4096,256]{0,1:T(8,128)}, f32[4096,256]{0,1:T(8,128)}, u32[]{:S(2)}, u32[]{:S(2)}) collective-permute-start(f32[4096,256]{0,1:T(8,128)} %all-reduce.14.cloned.1.call-done), channel_id=1, source_target_pairs={{0,8},{8,0},{16,24},{24,16},{1,9},{9,1},{17,25},{25,17},{2,10},{10... | collective-permute-start | bytes 12582920 | tf_op jit(solution)/shard_map/ppermute | solution.py:10
  435.4 3.4 copy-start.4
  462.5 472.1 %all-reduce.16.cloned.1.call-start = ((), (), s32[]{:S(2)}) async-start(), calls=%async_computation.3 | async-start | bytes 16777216 | tf_op jit(solution)/shard_map/psum | solution.py:107
  570.0 5.5 copy-start.6
  584.4 26.4 %collective-permute-start = (f32[1024,256]{1,0:T(8,128)}, f32[1024,256]{1,0:T(8,128)}, u32[]{:S(2)}, u32[]{:S(2)}) collective-permute-start(f32[1024,256]{1,0:T(8,128)} %bitcast.6), channel_id=1, source_target_pairs={{0,16},{8,24},{16,0},{24,8},{1,17},{9,25},{17,1},{25,9},{2,18},{10... | collective-permute-start | bytes 3145736 | tf_op jit(solution)/shard_map/ppermute | solution.py:10
  585.9 46.2 %collective-permute-start.3 = (f32[1024,256]{1,0:T(8,128)}, f32[1024,256]{1,0:T(8,128)}, u32[]{:S(2)}, u32[]{:S(2)}) collective-permute-start(f32[1024,256]{1,0:T(8,128)} %bitcast.138), channel_id=1, source_target_pairs={{0,16},{8,24},{16,0},{24,8},{1,17},{9,25},{17,1},{25,9},{2,18},{10... | collective-permute-start | bytes 3145736 | tf_op jit(solution)/shard_map/ppermute | solution.py:10
  643.6 660.4 %all-reduce.18.cloned.1.call-start = ((), (), s32[]{:S(2)}) async-start(), calls=%async_computation.4 | async-start | bytes 8388608 | tf_op jit(solution)/shard_map/psum | solution.py:18
  1125.6 14.5 copy-start.3
  1125.6 12.9 collective-permute-start.4
  1151.7 152.3 %copy-start.5 = (bf16[2,1024,256]{1,2,0:T(8,128)(2,1)S(1)}, bf16[2,1024,256]{1,2,0:T(8,128)(2,1)}, u32[]{:S(2)}) copy-start(bf16[2,1024,256]{1,2,0:T(8,128)(2,1)} %get-tuple-element.18) | copy-start | bytes 3145732
  1151.8 384.6 %all-reduce.20.cloned.1.call-start = ((), (), s32[]{:S(2)}) async-start(), calls=%async_computation.6 | async-start | bytes 8388608 | tf_op jit(solution)/shard_map/psum | solution.py:18
  1304.1 7.5 collective-permute-start.5
  1351.8 14.9 copy-start.2
  1351.8 14.9 collective-permute-start.6
  1383.0 197.3 %reduce-scatter.2.cloned.1.call-start = ((), (), s32[]{:S(2)}) async-start(), calls=%async_computation.5 | async-start | bytes 3145728 | tf_op jit(solution)/shard_map/reduce_scatter | solution.py:128
  1536.3 46.5 %copy-start.1 = (bf16[1,2048,256]{2,1,0:T(8,128)(2,1)S(1)}, bf16[1,2048,256]{2,1,0:T(8,128)(2,1)}, u32[]{:S(2)}) copy-start(bf16[1,2048,256]{2,1,0:T(8,128)(2,1)} %param.16) | copy-start | bytes 3145732
Sparse Core Ops, SparseCore 0:
  184.2 61.8 all-reduce.11
  266.8 154.9 all-reduce.13
  462.6 107.3 all-reduce.21
  643.7 290.8 all-reduce.15
  1151.9 152.1 all-reduce.17
  1383.2 153.1 all-reduce.19
  1549.4 30.8 reduce-scatter.1
